TPU v7x, 32 devices: a whole 2x2x4 slice. The times are simulated.
32 devices in a mesh: rt: 8 (over y, x, core), ct: 4 (over z).
Axes of the slice: x: 2, y: 2, z: 4, core: 2. Of those that a mesh axis runs over, the one named last changes fastest.
Arguments:
- factor_rows: float32 [48, 2, 1024, 1024], P('rt', None, 'ct'), as said below
- slot_row: int32 [48], replicated, may hold values from -1 to 31, as said below
- known: float32 [48, 1024, 256], P('rt', 'ct'), may hold values from -6 to 6
- rhs: float32 [2, 1024, 256], P(None, 'ct', 'rt'), may hold values from -6 to 6
Outputs:
- solved: float32 [2, 1024, 256], P(None, 'ct', 'rt')
Inputs may be any that keep to these rules, and one draw needn't show every extreme that they name: `slot_row`: each row tile 0 to 31 stands in exactly one slot; the other slots hold -1. The slots of one index of rt are the 6 consecutive ones; at most 6 are live, and some index of rt has all 6 live. `factor_rows`: diagonal tiles L[0, 0] and L[1, 1] are lower triangular with diagonal entries from 1 to 2; the entry block (0, 1) is zero; entries of empty slots are arbitrary.
All inputs are finite; a program needn't handle non-finite values.
Results may differ from a plain program's by a relative error of at most 0.0003.
Values sent between devices are 32-bit elements; how exact they have to be, the bound alone decides.
No kernel may reach another device: no remote copies, remote signals or barrier semaphores. Data moves between devices by JAX's collectives and lax.ppermute only.
A program may use at most 64 MiB of HBM per device.

v0:
```python
import jax
import jax.numpy as jnp
from jax import lax
from jax.sharding import PartitionSpec as P


def spread(value, axis, root):
    mine = lax.axis_index(axis) == root
    return lax.psum(jnp.where(mine, value, jnp.zeros_like(value)), axis)


def shards(factor_rows, slot_row, known, rhs):
    high = lax.Precision.HIGHEST
    band = known.shape[1]
    columns = rhs.shape[2]
    slot_count = factor_rows.shape[0]
    offset = lax.axis_index("ct") * band
    col_offset = lax.axis_index("rt") * columns
    local_rows = lax.dynamic_slice_in_dim(
        slot_row, lax.axis_index("rt") * slot_count, slot_count, 0
    )
    live = (local_rows >= 2).astype(jnp.float32)
    masked = known * live[:, None, None]
    partial_value = jnp.einsum("scka,skr->car", factor_rows, masked, precision=high)
    pick_zero = local_rows == 0
    pick_one = local_rows == 1
    diag_zero = jnp.sum(jnp.where(pick_zero[:, None, None], factor_rows[:, 0], 0.0), 0)
    diag_one = jnp.sum(jnp.where(pick_one[:, None, None], factor_rows[:, 1], 0.0), 0)
    lower_one = jnp.sum(jnp.where(pick_one[:, None, None], factor_rows[:, 0], 0.0), 0)
    owner_zero = jnp.argmax(slot_row == 0) // slot_count
    owner_one = jnp.argmax(slot_row == 1) // slot_count
    tile_zero = spread(diag_zero, "rt", owner_zero)
    tile_one, tile_lower = (spread(diag_one, "rt", owner_one), spread(lower_one, "rt", owner_one))
    total = lax.psum(partial_value, ("rt", "ct"))
    rows_mine = lax.dynamic_slice_in_dim(total, offset, band, 1)
    mine = lax.dynamic_slice_in_dim(rows_mine, col_offset, columns, 2)
    residual = lax.all_gather(rhs - mine, "ct", axis=1, tiled=True)
    whole_zero, whole_one = (
        lax.all_gather(tile_zero, "ct", axis=0, tiled=True),
        lax.all_gather(tile_one, "ct", axis=0, tiled=True),
    )
    solved_one = lax.linalg.triangular_solve(
        whole_one, residual[1], left_side=True, lower=True, transpose_a=True
    )
    one_band = lax.dynamic_slice_in_dim(solved_one, offset, band, 0)
    coupling = jnp.einsum("ka,kr->ar", tile_lower, one_band, precision=high)
    coupled = lax.psum(coupling, "ct")
    solved_zero = lax.linalg.triangular_solve(
        whole_zero, residual[0] - coupled, left_side=True, lower=True, transpose_a=True
    )
    zero_band = lax.dynamic_slice_in_dim(solved_zero, offset, band, 0)
    return jnp.stack([zero_band, one_band])


def solution(mesh):
    in_specs = (P("rt", None, "ct", None), P(), P("rt", "ct", None), P(None, "ct", "rt"))
    out_specs = P(None, "ct", "rt")
    return jax.shard_map(shards, mesh=mesh, in_specs=in_specs, out_specs=out_specs, check_vma=False)
```

profile of v0, /device:TPU:0, one launch (start us, length us, event | category | flops | bytes accessed | tf_op | source)
XLA Modules:
  0.0 562.1 jit_solution(5160775739267857526)
XLA Ops:
  14.2 6.1 %fusion.2 = (f32[256,1024]{1,0:T(8,128)S(1)}, f32[256,1024]{1,0:T(8,128)S(1)}, f32[256,1024]{1,0:T(8,128)S(1)}) fusion(f32[6,2,256,1024]{3,2,1,0:T(8,128)} %param.6, pred[6]{0:T(512)(128)(4,1)S(1)} %get-tuple-element.53, pred[6]{0:T(512)(128)(4,1)S(1)} %get-tuple-element.54), kind=kLoop, calls=%fused_computation.9 | loop fusion | flops 8650752 | bytes 15728652 | tf_op jit(solution)/shard_map/reduce_sum | solution.py:29
  23.3 14.9 %convolution_bitcast_fusion = f32[2,1024,256]{1,2,0:T(8,128)} fusion(f32[6,2,256,1024]{3,2,1,0:T(8,128)} %param.6, f32[6,256,256]{2,1,0:T(8,128)S(1)} %copy-done, f32[6]{0:T(128)S(1)} %get-tuple-element.52), kind=kOutput, calls=%fused_computation.13 | convolution fusion | flops 9664069632 | bytes 16252952 | tf_op jit(solution)/shard_map/scka,skr->car/dot_general | solution.py:24
  38.3 57.5 %all-reduce.9.cloned.1.call-done = (f32[256,1024]{1,0:T(8,128)}, f32[256,1024]{1,0:T(8,128)}, f32[256,1024]{1,0:T(8,128)}) async-done(((f32[256,1024]{1,0:T(8,128)}, f32[256,1024]{1,0:T(8,128)}, f32[256,1024]{1,0:T(8,128)}), (f32[256,1024]{1,0:T(8,128)}, f32[256,1024]{1,0:T(8,128)}, f32[256,1024]{1,0:T(8,128)})) %all-reduce.9.cloned.1.call-update) | async-done | bytes 3145744 | tf_op jit(solution)/shard_map/psum | solution.py:9
  95.9 140.0 %all-reduce.5.cloned.1.call-done = f32[2,1024,256]{1,2,0:T(8,128)} async-done(((f32[2,1024,256]{1,2,0:T(8,128)}), f32[2,1024,256]{1,2,0:T(8,128)}) %all-reduce.5.cloned.1.call-update) | async-done | bytes 2097168 | tf_op jit(solution)/shard_map/psum | solution.py:34
  236.9 14.7 %all_gather.10 = f32[2,1024,32]{1,2,0:T(8,128)S(1)} all-gather(f32[2,256,32]{1,2,0:T(8,128)S(1)} %dynamic-slice_subtract_fusion), channel_id=1, replica_groups=mesh['rt'=8,'ct'=4] {'ct'}, dimensions={1}, use_global_device_ids=true | all-gather | bytes 327680 | tf_op jit(solution)/shard_map/all_gather | solution.py:37
  251.8 66.0 %all-gather.5.cloned.1.call-done = f32[1024,1024]{1,0:T(8,128)} async-done(((f32[256,1024]{1,0:T(8,128)}), f32[1024,1024]{1,0:T(8,128)}) %all-gather.5.cloned.1.call-update) | async-done | bytes 4194320 | tf_op jit(solution)/shard_map/all_gather | solution.py:40
  317.8 4.7 fusion.3
  322.6 22.5 %while.4 = (s32[]{:T(128)}, f32[1024,1024]{1,0:T(8,128)}, s32[8,2]{0,1:T(2,128)S(1)}, f32[8,128,128]{2,1,0:T(8,128)S(1)}, s32[]{:T(128)}) while((s32[]{:T(128)}, f32[1024,1024]{1,0:T(8,128)}, s32[8,2]{0,1:T(2,128)S(1)}, f32[8,128,128]{2,1,0:T(8,128)S(1)}, s32[]{:T(128)}) %tuple.49), condition=%wide.while_cond, body=%wide.while_body.sunk | while | flops 2 | bytes 131181 | solution.py:42
  323.2 2.2 bitcast_dynamic-update-slice_fusion.4
  326.1 2.2 bitcast_dynamic-update-slice_fusion.4
  331.7 2.2 bitcast_dynamic-update-slice_fusion.4
  337.3 2.2 bitcast_dynamic-update-slice_fusion.4
  345.1 78.6 %custom-call.4 = f32[8,128,128]{1,2,0:T(8,128)S(1)} custom-call(f32[8,128,128]{2,1,0:T(8,128)S(1)} %get-tuple-element.24), custom_call_target="InvertDiagBlocksLowerTriangular" | custom-call | tf_op jit(solution)/shard_map/triangular_solve/custom-call.1 | solution.py:42
  435.8 4.7 fusion.4
  440.5 24.2 %while.5 = (s32[]{:T(128)}, f32[1024,1024]{1,0:T(8,128)}, s32[8,2]{0,1:T(2,128)S(1)}, f32[8,128,128]{2,1,0:T(8,128)S(1)}, s32[]{:T(128)}) while((s32[]{:T(128)}, f32[1024,1024]{1,0:T(8,128)}, s32[8,2]{0,1:T(2,128)S(1)}, f32[8,128,128]{2,1,0:T(8,128)S(1)}, s32[]{:T(128)}) %tuple.66), condition=%wide.while_cond.clone, body=%wide.while_body.clone.sunk | while | flops 2 | bytes 131181 | solution.py:48
  441.2 2.3 bitcast_dynamic-update-slice_fusion.5
  444.2 2.3 bitcast_dynamic-update-slice_fusion.5
  447.3 2.3 bitcast_dynamic-update-slice_fusion.5
  450.3 2.3 bitcast_dynamic-update-slice_fusion.5
  453.3 2.3 bitcast_dynamic-update-slice_fusion.5
  456.4 2.3 bitcast_dynamic-update-slice_fusion.5
  459.4 2.3 bitcast_dynamic-update-slice_fusion.5
  462.4 2.3 bitcast_dynamic-update-slice_fusion.5
  464.7 78.6 %custom-call.5 = f32[8,128,128]{1,2,0:T(8,128)S(1)} custom-call(f32[8,128,128]{2,1,0:T(8,128)S(1)} %get-tuple-element.25), custom_call_target="InvertDiagBlocksLowerTriangular" | custom-call | tf_op jit(solution)/shard_map/triangular_solve/custom-call.1 | solution.py:48
  (144 shorter events, 50.4 us)
Async XLA Ops:
  6.5 89.3 %all-reduce.9.cloned.1.call-start = ((), (), s32[]{:S(2)}) async-start(), calls=%async_computation.4 | async-start | bytes 6291456 | tf_op jit(solution)/shard_map/psum | solution.py:9
  21.4 1.9 copy-start
  23.1 212.8 %all-reduce.5.cloned.1.call-start = ((), (), s32[]{:S(2)}) async-start(), calls=%async_computation.1 | async-start | bytes 4194304 | tf_op jit(solution)/shard_map/psum | solution.py:34
  23.3 212.6 %copy-start.2 = (f32[2,256,32]{1,2,0:T(8,128)S(1)}, f32[2,256,32]{1,2,0:T(8,128)}, u32[]{:S(2)}) copy-start(f32[2,256,32]{1,2,0:T(8,128)} %param.9) | copy-start | bytes 196612
  38.2 279.6 %all-gather.5.cloned.1.call-start = ((), (), s32[]{:S(2)}) async-start(), calls=%async_computation.2 | async-start | bytes 5242880 | tf_op jit(solution)/shard_map/all_gather | solution.py:40
  95.8 339.9 %all-gather.3.cloned.1.call-start = ((), (), s32[]{:S(2)}) async-start(), calls=%async_computation | async-start | bytes 5242880 | tf_op jit(solution)/shard_map/all_gather | solution.py:39
  251.6 291.7 %all-reduce.7.cloned.1.call-start = ((), (), s32[]{:S(2)}) async-start(), calls=%async_computation.3 | async-start | bytes 262144 | tf_op jit(solution)/shard_map/psum | solution.py:47
  322.6 111.8 %copy-start.1 = (f32[256,1024]{1,0:T(8,128)S(1)}, f32[256,1024]{1,0:T(8,128)}, u32[]{:S(2)}) copy-start(f32[256,1024]{1,0:T(8,128)} %get-tuple-element.47) | copy-start | bytes 3145732
Sparse Core Ops, SparseCore 0:
  23.2 72.5 all-reduce.8
  102.0 133.8 all-reduce.4
  237.5 80.3 all-gather.4
  319.2 79.3 all-gather.2
  435.9 33.0 all-reduce.6
where the time goes:
time: 564 us; the launch traced here: 562 us
  waiting for transfers between devices  264 us (47%)
  other arithmetic  182 us (32%)
  local copies, waits for them, and re-layouts  47 us (8%)
  matrix products  36.6 us (6%)
  between operations  18 us (3%)
  blocking collectives  14.7 us (3%)
    psum x1, waiting for transfers between devices, shards(): total = lax.psum(partial_value, ('rt', 'ct'))  140 us
    another operation x3, other arithmetic, shards(): lax.linalg.triangular_solve(whole_zero, residual[0] - coupled, left_side=...  83.3 us
    another operation x2, other arithmetic, shards(): lax.linalg.triangular_solve(whole_one, residual[1], left_side=True, lower...  83.3 us
    all_gather x1, waiting for transfers between devices, shards(): lax.all_gather(tile_one, 'ct', axis=0, tiled=True)  66 us
    psum x1, waiting for transfers between devices, spread(): return lax.psum(jnp.where(mine, value, jnp.zeros_like(value)), axis)  57.5 us
    another operation x31, local copies, waits for them, and re-layouts, shards(): lax.linalg.triangular_solve(whole_zero, residual[0] - coupled, left_side=...  24.1 us
    another operation x28, local copies, waits for them, and re-layouts, shards(): lax.linalg.triangular_solve(whole_one, residual[1], left_side=True, lower...  22.4 us
    dot_general x1, matrix products, shards(): jnp.einsum('scka,skr->car', factor_rows, masked, precision=high)  14.9 us
  transfers between devices with their start and end apart: 5, of which 3 were waited for; matrix products, arithmetic and copies ran while one was open for 43% of the time, Pallas kernels for 0%

commit v1 on v0

--- a/solution.py
+++ b/solution.py
@@ -34,7 +34,22 @@
     total = lax.psum(partial_value, ("rt", "ct"))
     rows_mine = lax.dynamic_slice_in_dim(total, offset, band, 1)
     mine = lax.dynamic_slice_in_dim(rows_mine, col_offset, columns, 2)
-    residual = lax.all_gather(rhs - mine, "ct", axis=1, tiled=True)
+    shard = rhs - mine
+    ways, here, lap = (lax.axis_size("ct"), lax.axis_index("ct"), shard.shape[1])
+    lengths = [n * ways if d == 1 else n for d, n in enumerate(shard.shape)]
+    full = lax.dynamic_update_slice_in_dim(
+        jnp.zeros(lengths, shard.dtype), shard, here * lap, axis=1
+    )
+    going_up = going_down = shard
+    for far in range(1, ways // 2 + 1):
+        going_up = lax.ppermute(going_up, "ct", [(d, (d + 1) % ways) for d in range(ways)])
+        full = lax.dynamic_update_slice_in_dim(full, going_up, (here - far) % ways * lap, axis=1)
+        if 2 * far < ways:
+            going_down = lax.ppermute(going_down, "ct", [(d, (d - 1) % ways) for d in range(ways)])
+            full = lax.dynamic_update_slice_in_dim(
+                full, going_down, (here + far) % ways * lap, axis=1
+            )
+    residual = full
     whole_zero, whole_one = (
         lax.all_gather(tile_zero, "ct", axis=0, tiled=True),
         lax.all_gather(tile_one, "ct", axis=0, tiled=True),

time: 564 us -> 563 us (level)
  blocking collectives: 14.7 us -> 0 us
  waiting for transfers between devices: 264 us -> 274 us
    all_gather x1 -> x0, blocking collectives: 14.7 us -> none  [shards(): residual = lax.all_gather(rhs - mine, 'ct', axis=1, tiled=True)]
    ppermute x0 -> x3, waiting for transfers between devices: none -> 8.51 us  [the longest x2 8.48 us: shards(): lax.ppermute(going_up, 'ct', [(d, (d + 1) % ways) for d in range(ways)])]
  transfers between devices with their start and end apart: 5 -> 8, of which waited for: 3 -> 5; matrix products, arithmetic and copies ran while one was open for 43% -> 43% of each run, Pallas kernels for 0% -> 0%
where the time goes in v1:
time: 563 us; the launch traced here: 562 us
  waiting for transfers between devices  274 us (49%)
  other arithmetic  182 us (32%)
  local copies, waits for them, and re-layouts  47 us (8%)
  matrix products  36.6 us (7%)
  between operations  18.1 us (3%)
    psum x1, waiting for transfers between devices, shards(): total = lax.psum(partial_value, ('rt', 'ct'))  140 us
    another operation x3, other arithmetic, shards(): lax.linalg.triangular_solve(whole_zero, residual[0] - coupled, left_side=...  83.3 us
    another operation x2, other arithmetic, shards(): lax.linalg.triangular_solve(whole_one, residual[1], left_side=True, lower...  83.3 us
    all_gather x1, waiting for transfers between devices, shards(): lax.all_gather(tile_one, 'ct', axis=0, tiled=True)  67.8 us
    psum x1, waiting for transfers between devices, spread(): return lax.psum(jnp.where(mine, value, jnp.zeros_like(value)), axis)  57.5 us
    another operation x31, local copies, waits for them, and re-layouts, shards(): lax.linalg.triangular_solve(whole_zero, residual[0] - coupled, left_side=...  24.1 us
    another operation x28, local copies, waits for them, and re-layouts, shards(): lax.linalg.triangular_solve(whole_one, residual[1], left_side=True, lower...  22.4 us
    dot_general x1, matrix products, shards(): jnp.einsum('scka,skr->car', factor_rows, masked, precision=high)  14.9 us
  transfers between devices with their start and end apart: 8, of which 5 were waited for; matrix products, arithmetic and copies ran while one was open for 43% of the time, Pallas kernels for 0%

profile of v1, /device:TPU:0, one launch (start us, length us, event | category | flops | bytes accessed | tf_op | source)
XLA Modules:
  0.0 561.7 jit_solution(18231705297164485665)
XLA Ops:
  14.2 6.1 %fusion.2 = (f32[256,1024]{1,0:T(8,128)S(1)}, f32[256,1024]{1,0:T(8,128)S(1)}, f32[256,1024]{1,0:T(8,128)S(1)}) fusion(f32[6,2,256,1024]{3,2,1,0:T(8,128)} %param.6, pred[6]{0:T(512)(128)(4,1)S(1)} %get-tuple-element.55, pred[6]{0:T(512)(128)(4,1)S(1)} %get-tuple-element.56), kind=kLoop, calls=%fused_computation.9 | loop fusion | flops 8650752 | bytes 15728652 | tf_op jit(solution)/shard_map/reduce_sum | solution.py:29
  23.3 14.9 %convolution_bitcast_fusion = f32[2,1024,256]{1,2,0:T(8,128)} fusion(f32[6,2,256,1024]{3,2,1,0:T(8,128)} %param.6, f32[6,256,256]{2,1,0:T(8,128)S(1)} %copy-done, f32[6]{0:T(128)S(1)} %get-tuple-element.54), kind=kOutput, calls=%fused_computation.13 | convolution fusion | flops 9664069632 | bytes 16252952 | tf_op jit(solution)/shard_map/scka,skr->car/dot_general | solution.py:24
  38.3 57.5 %all-reduce.9.cloned.1.call-done = (f32[256,1024]{1,0:T(8,128)}, f32[256,1024]{1,0:T(8,128)}, f32[256,1024]{1,0:T(8,128)}) async-done(((f32[256,1024]{1,0:T(8,128)}, f32[256,1024]{1,0:T(8,128)}, f32[256,1024]{1,0:T(8,128)}), (f32[256,1024]{1,0:T(8,128)}, f32[256,1024]{1,0:T(8,128)}, f32[256,1024]{1,0:T(8,128)})) %all-reduce.9.cloned.1.call-update) | async-done | bytes 3145744 | tf_op jit(solution)/shard_map/psum | solution.py:9
  96.0 139.9 %all-reduce.5.cloned.1.call-done = f32[2,1024,256]{1,2,0:T(8,128)} async-done(((f32[2,1024,256]{1,2,0:T(8,128)}), f32[2,1024,256]{1,2,0:T(8,128)}) %all-reduce.5.cloned.1.call-update) | async-done | bytes 2097168 | tf_op jit(solution)/shard_map/psum | solution.py:34
  238.3 2.5 collective-permute-start.1
  240.8 2.4 collective-permute-done
  243.3 6.1 %collective-permute-done.2 = f32[2,256,32]{1,2,0:T(8,128)S(1)} collective-permute-done((f32[2,256,32]{1,2,0:T(8,128)S(1)}, f32[2,256,32]{1,2,0:T(8,128)S(1)}, u32[]{:S(2)}, u32[]{:S(2)}) %collective-permute-start.2) | collective-permute-done | bytes 65568 | tf_op jit(solution)/shard_map/ppermute | solution.py:45
  249.7 67.8 %all-gather.5.cloned.1.call-done = f32[1024,1024]{1,0:T(8,128)} async-done(((f32[256,1024]{1,0:T(8,128)}), f32[1024,1024]{1,0:T(8,128)}) %all-gather.5.cloned.1.call-update) | async-done | bytes 4194320 | tf_op jit(solution)/shard_map/all_gather | solution.py:55
  317.5 4.7 fusion.3
  322.3 22.5 %while.4 = (s32[]{:T(128)}, f32[1024,1024]{1,0:T(8,128)}, s32[8,2]{0,1:T(2,128)S(1)}, f32[8,128,128]{2,1,0:T(8,128)S(1)}, s32[]{:T(128)}) while((s32[]{:T(128)}, f32[1024,1024]{1,0:T(8,128)}, s32[8,2]{0,1:T(2,128)S(1)}, f32[8,128,128]{2,1,0:T(8,128)S(1)}, s32[]{:T(128)}) %tuple.50), condition=%wide.while_cond, body=%wide.while_body.sunk | while | flops 2 | bytes 131181 | solution.py:57
  322.9 2.2 bitcast_dynamic-update-slice_fusion.4
  325.7 2.2 bitcast_dynamic-update-slice_fusion.4
  344.8 78.6 %custom-call.4 = f32[8,128,128]{1,2,0:T(8,128)S(1)} custom-call(f32[8,128,128]{2,1,0:T(8,128)S(1)} %get-tuple-element.24), custom_call_target="InvertDiagBlocksLowerTriangular" | custom-call | tf_op jit(solution)/shard_map/triangular_solve/custom-call.1 | solution.py:57
  435.4 4.7 fusion.4
  440.2 24.2 %while.5 = (s32[]{:T(128)}, f32[1024,1024]{1,0:T(8,128)}, s32[8,2]{0,1:T(2,128)S(1)}, f32[8,128,128]{2,1,0:T(8,128)S(1)}, s32[]{:T(128)}) while((s32[]{:T(128)}, f32[1024,1024]{1,0:T(8,128)}, s32[8,2]{0,1:T(2,128)S(1)}, f32[8,128,128]{2,1,0:T(8,128)S(1)}, s32[]{:T(128)}) %tuple.67), condition=%wide.while_cond.clone, body=%wide.while_body.clone.sunk | while | flops 2 | bytes 131181 | solution.py:63
  440.9 2.3 bitcast_dynamic-update-slice_fusion.5
  443.9 2.3 bitcast_dynamic-update-slice_fusion.5
  446.9 2.3 bitcast_dynamic-update-slice_fusion.5
  450.0 2.3 bitcast_dynamic-update-slice_fusion.5
  453.0 2.3 bitcast_dynamic-update-slice_fusion.5
  456.0 2.3 bitcast_dynamic-update-slice_fusion.5
  459.1 2.3 bitcast_dynamic-update-slice_fusion.5
  462.1 2.3 bitcast_dynamic-update-slice_fusion.5
  464.4 78.6 %custom-call.5 = f32[8,128,128]{1,2,0:T(8,128)S(1)} custom-call(f32[8,128,128]{2,1,0:T(8,128)S(1)} %get-tuple-element.25), custom_call_target="InvertDiagBlocksLowerTriangular" | custom-call | tf_op jit(solution)/shard_map/triangular_solve/custom-call.1 | solution.py:63
  (153 shorter events, 56.4 us)
Async XLA Ops:
  6.5 89.3 %all-reduce.9.cloned.1.call-start = ((), (), s32[]{:S(2)}) async-start(), calls=%async_computation.4 | async-start | bytes 6291456 | tf_op jit(solution)/shard_map/psum | solution.py:9
  21.4 1.9 copy-start
  23.1 212.8 %all-reduce.5.cloned.1.call-start = ((), (), s32[]{:S(2)}) async-start(), calls=%async_computation.1 | async-start | bytes 4194304 | tf_op jit(solution)/shard_map/psum | solution.py:34
  23.3 212.6 %copy-start.2 = (f32[2,256,32]{1,2,0:T(8,128)S(1)}, f32[2,256,32]{1,2,0:T(8,128)}, u32[]{:S(2)}) copy-start(f32[2,256,32]{1,2,0:T(8,128)} %param.9) | copy-start | bytes 196612
  38.2 279.3 %all-gather.5.cloned.1.call-start = ((), (), s32[]{:S(2)}) async-start(), calls=%async_computation.2 | async-start | bytes 5242880 | tf_op jit(solution)/shard_map/all_gather | solution.py:55
  95.8 339.6 %all-gather.3.cloned.1.call-start = ((), (), s32[]{:S(2)}) async-start(), calls=%async_computation | async-start | bytes 5242880 | tf_op jit(solution)/shard_map/all_gather | solution.py:54
  236.9 6.3 %collective-permute-start = (f32[2,256,32]{1,2,0:T(8,128)S(1)}, f32[2,256,32]{1,2,0:T(8,128)S(1)}, u32[]{:S(2)}, u32[]{:S(2)}) collective-permute-start(f32[2,256,32]{1,2,0:T(8,128)S(1)} %get-tuple-element.49), channel_id=1, source_target_pairs={{0,1},{1,2},{2,3},{3,0},{4,5},{5,6},{6,7},{7,4},{8,9},{9,10},{10,1... | collective-permute-start | bytes 196616 | tf_op jit(solution)/shard_map/ppermute | solution.py:45
  238.3 5.0 collective-permute-start.1
  243.2 6.2 %collective-permute-start.2 = (f32[2,256,32]{1,2,0:T(8,128)S(1)}, f32[2,256,32]{1,2,0:T(8,128)S(1)}, u32[]{:S(2)}, u32[]{:S(2)}) collective-permute-start(f32[2,256,32]{1,2,0:T(8,128)S(1)} %collective-permute-done), channel_id=1, source_target_pairs={{0,1},{1,2},{2,3},{3,0},{4,5},{5,6},{6,7},{7,4},{8,9},{9,10},{10,1... | collective-permute-start | bytes 196616 | tf_op jit(solution)/shard_map/ppermute | solution.py:45
  249.5 293.5 %all-reduce.7.cloned.1.call-start = ((), (), s32[]{:S(2)}) async-start(), calls=%async_computation.3 | async-start | bytes 262144 | tf_op jit(solution)/shard_map/psum | solution.py:62
  322.2 111.8 %copy-start.1 = (f32[256,1024]{1,0:T(8,128)S(1)}, f32[256,1024]{1,0:T(8,128)}, u32[]{:S(2)}) copy-start(f32[256,1024]{1,0:T(8,128)} %get-tuple-element.47) | copy-start | bytes 3145732
Sparse Core Ops, SparseCore 0:
  23.2 72.5 all-reduce.8
  102.0 133.8 all-reduce.4
  237.5 79.9 all-gather.4
  318.9 78.9 all-gather.2
  435.5 32.6 all-reduce.6
